TPU v7x, 32 devices: a whole 2x2x4 slice. The times are simulated.
32 devices in a mesh: section: 16 (over z, y, core), dp: 2 (over x).
Axes of the slice: x: 2, y: 2, z: 4, core: 2. Of those that a mesh axis runs over, the one named last changes fastest.
Arguments:
- activations: bfloat16 [16, 16, 64, 4096], P('section', 'dp'), may hold values from -6 to 6
- out_grads: bfloat16 [16, 16, 64, 4096], P('section', 'dp'), may hold values from -6 to 6
- proj_in: bfloat16 [16, 2, 4096, 128], P('section'), may hold values from -0.09375 to 0.09375
- proj_out: bfloat16 [16, 2, 64, 4096], P('section'), may hold values from -0.09375 to 0.09375
- earlier_gram: float32 [8192, 8192], P('section', 'dp'), may hold values from -4 to 4, as said below
Outputs:
- gram: float32 [8192, 8192], P('section', 'dp')
Inputs may be any that keep to these rules, and one draw needn't show every extreme that they name: earlier_gram is symmetric.
All inputs are finite; a program needn't handle non-finite values.
Results may differ from a plain program's by a relative error of at most 0.0013.
Values sent between devices are 32-bit elements; how exact they have to be, the bound alone decides.
A program may use at most 64 MiB of HBM per device.

v0:
```python
import functools
import math

import jax
import jax.numpy as jnp
from jax import lax
from jax.experimental import pallas as pl
from jax.experimental.pallas import tpu as pltpu
from jax.sharding import PartitionSpec as P

MESH = pl.DeviceIdType.MESH
LANES = 128
HALVES = 2
DEPTHS = 1
WINDOW = 4


def split(x):
    hi = x.astype(jnp.bfloat16)
    lo = (x - hi.astype(jnp.float32)).astype(jnp.bfloat16)
    return hi, lo


def feature_kernel(
    n, groups, count, scale,
    act, grad, p_in, p_out, earlier,
    left, right, held,
    act_v, grad_v, in_v, out_v, low_in, low_out,
    mine, theirs, arrived, pieces, own, cols, row,
    load_sem, pair_sem, send_sem, recv_sem,
    col_send, col_recv, fwd_send, row_send, row_recv, held_sem,
):
    s = lax.axis_index("section")
    d = lax.axis_index("dp")
    chips = n // 2
    core = s % 2
    chip = s // 2
    partner = s + 1 - 2 * core

    draws, width, k_in = p_in.shape
    k_out = p_out.shape[1]
    tokens = act.shape[0]
    length = tokens // count
    rows = tokens // HALVES
    depth = width // DEPTHS

    loads = {}
    slot = 0
    for h in range(HALVES):
        for c in range(DEPTHS):
            cs = pl.ds(c * depth, depth)
            rs = pl.ds(h * rows, rows)
            wanted = []
            if h == 0:
                wanted.append(("p_in", p_in.at[:, cs], in_v.at[:, cs]))
            wanted.append(("act", act.at[rs, cs], act_v.at[rs, cs]))
            if h == 0:
                wanted.append(("p_out", p_out.at[:, :, cs], out_v.at[:, :, cs]))
            wanted.append(("grad", grad.at[rs, cs], grad_v.at[rs, cs]))
            for name, src, dst in wanted:
                copy = pltpu.make_async_copy(src, dst, load_sem.at[slot])
                loads[name, h, c] = copy
                slot += 1
    queue = list(loads.values())

    def take(copy):
        copy.wait()
        if queue:
            queue.pop(0).start()

    for _ in range(WINDOW):
        queue.pop(0).start()

    barrier = pltpu.get_barrier_semaphore()
    for g in range(groups):
        for i in range(n):
            if g or i:
                peer = {"section": (s + i) % n, "dp": (d + g) % groups}
                pl.semaphore_signal(barrier, inc=1, device_id=peer, device_id_type=MESH)

    for h in range(HALVES):
        rs = slice(h * rows, (h + 1) * rows)
        total_in = total_out = None
        for c in range(DEPTHS):
            cs = slice(c * depth, (c + 1) * depth)
            if h == 0:
                take(loads["p_in", h, c])
            take(loads["act", h, c])
            weights = jnp.concatenate([in_v[p, cs, :] for p in range(draws)], axis=1)
            term = jnp.dot(act_v[rs, cs], weights, preferred_element_type=jnp.float32)
            total_in = term if total_in is None else total_in + term
            if h == 0:
                take(loads["p_out", h, c])
            take(loads["grad", h, c])
            weights = out_v[:, :, cs].reshape(draws * k_out, depth)
            term = lax.dot_general(
                grad_v[rs, cs], weights, (((1,), (1,)), ((), ())), preferred_element_type=jnp.float32
            )
            total_out = term if total_out is None else total_out + term
        if h == HALVES - 1:
            hold = pltpu.make_async_copy(earlier, held, held_sem)
            hold.start()
        low_in[rs, :] = total_in.astype(jnp.bfloat16)
        low_out[:, rs] = total_out.T.astype(jnp.bfloat16)

    k_half = k_out // 2

    def terms(which, into):
        for e in range(count):
            ts = slice(e * length, (e + 1) * length)
            value = None
            for p in range(draws):
                start = pl.multiple_of(p * k_out + which * k_half, k_half)
                term = jnp.dot(
                    low_out[pl.ds(start, k_half), ts],
                    low_in[ts, p * k_in:(p + 1) * k_in],
                    preferred_element_type=jnp.float32,
                )
                value = term if value is None else value + term
            into[:, e, :] = value

    def remote(src, dst, ssem, rsem, section, dp):
        return pltpu.make_async_remote_copy(
            src_ref=src, dst_ref=dst, send_sem=ssem, recv_sem=rsem,
            device_id={"section": section, "dp": dp}, device_id_type=MESH,
        )

    terms(1 - core, theirs)
    pl.semaphore_wait(barrier, n * groups - 1)
    swap = remote(theirs, arrived, pair_sem.at[0], pair_sem.at[1], partner, d)
    swap.start()
    terms(core, mine)
    swap.wait_recv()

    def across(c, i):
        bit = 1
        while bit < chips:
            if i & bit:
                c = c + bit * (1 - 2 * ((c // bit) % 2))
            bit *= 2
        return c

    k_chunk = k_half // chips
    sends = []
    for i in range(chips - 1, 0, -1):
        to = across(chip, i)
        ks = pl.ds(to * k_chunk, k_chunk)
        mine[ks] = mine[ks] + arrived[ks]
        copy = remote(mine.at[ks], pieces.at[i - 1], send_sem.at[i - 1], recv_sem.at[i - 1], 2 * to + core, d)
        copy.start()
        sends.append(copy)
    ks = pl.ds(chip * k_chunk, k_chunk)
    total = mine[ks] + arrived[ks]
    for i in range(1, chips):
        sends[chips - 1 - i].wait_recv()
        total = total + pieces[i - 1]

    own[...] = total

    per_group = n // groups
    q = core * chips + chip
    own_slot = q % per_group
    home = q // per_group
    at_home = home == d

    def col_copy(i):
        return remote(
            own, cols.at[own_slot, d], col_send.at[i], col_recv.at[own_slot, d], 2 * across(chip, i) + core, home
        )

    def pair_copy():
        return remote(own, cols.at[own_slot, d], col_send.at[0], col_recv.at[own_slot, d], partner, d)

    def row_copy(g):
        return remote(own, row.at[d], row_send.at[g], row_recv.at[d], q, g)

    for i in range(chips - 1, 0, -1):
        col_copy(i).start()

    @pl.when(at_home)
    def _():
        pair_copy().start()
        cols[own_slot, d] = own[...]

    @pl.when(jnp.logical_not(at_home))
    def _():
        col_copy(0).start()

    for g in range(groups):
        needed = home != g
        here = jnp.logical_and(q == s, d == g)

        @pl.when(jnp.logical_and(needed, jnp.logical_not(here)))
        def _():
            row_copy(g).start()

        @pl.when(jnp.logical_and(needed, here))
        def _():
            row[d] = own[...]

    def forward(j, g):
        return remote(cols.at[j, g], cols.at[j, g], fwd_send.at[j, g], col_recv.at[j, g], partner, d)

    for i in range(per_group):
        j = across(chip, i) % per_group
        owner = d * per_group + j
        for g in range(groups):
            other = jnp.logical_or(owner != q, d != g)

            @pl.when(other)
            def _():
                forward(j, g).wait_recv()

            @pl.when(jnp.logical_and(other, owner // chips == core))
            def _():
                forward(j, g).start()

        for k in range(k_chunk):
            hi, lo = split(jnp.concatenate([cols[j, g, k] for g in range(groups)], axis=0))
            at = pl.multiple_of((j * k_chunk + k) * LANES, LANES)
            right[:, pl.ds(at, LANES)] = jnp.concatenate([hi, hi, lo], axis=0)

    for g in range(groups):

        @pl.when(jnp.logical_and(s // per_group != d, jnp.logical_or(q != s, d != g)))
        def _():
            remote(own, row.at[g], row_send.at[g], row_recv.at[g], q, d).wait_recv()

    @pl.when(s // per_group == d)
    def _():
        row[...] = cols[s % per_group]

    for k in range(k_chunk):
        hi, lo = split(jnp.concatenate([row[g, k] for g in range(groups)], axis=0) * scale)
        left[:, k * LANES:(k + 1) * LANES] = jnp.concatenate([hi, lo, hi], axis=0)

    hold.wait()
    swap.wait_send()
    for copy in sends:
        copy.wait_send()

    for i in range(1, chips):
        col_copy(i).wait_send()

    @pl.when(at_home)
    def _():
        pair_copy().wait_send()

    @pl.when(jnp.logical_not(at_home))
    def _():
        col_copy(0).wait_send()

    for g in range(groups):

        @pl.when(jnp.logical_and(home != g, jnp.logical_or(q != s, d != g)))
        def _():
            row_copy(g).wait_send()

    for j in range(per_group):
        owner = d * per_group + j
        for g in range(groups):

            @pl.when(jnp.logical_and(jnp.logical_or(owner != q, d != g), owner // chips == core))
            def _():
                forward(j, g).wait_send()


def gram_kernel(tiles, left, right, earlier, out, tile_v, sem):
    columns = right.shape[1] // tiles
    lhs = left[...].T
    copies = []
    for i in range(tiles):
        cs = slice(i * columns, (i + 1) * columns)
        tile_v[:, cs] = earlier[:, cs] + jnp.dot(lhs, right[:, cs], preferred_element_type=jnp.float32)
        copy = pltpu.make_async_copy(
            tile_v.at[:, pl.ds(i * columns, columns)], out.at[:, pl.ds(i * columns, columns)], sem.at[i]
        )
        copy.start()
        copies.append(copy)
    for copy in copies:
        copy.wait()


def per_device(activations, out_grads, proj_in, proj_out, earlier_gram):
    n = lax.axis_size("section")
    groups = lax.axis_size("dp")
    _, count, length, width = activations.shape
    _, draws, _, k_in = proj_in.shape
    k_out = proj_out.shape[2]
    tokens = count * length
    examples = count * groups
    scale = 1.0 / (length * n * draws) / examples
    row_width, col_width = earlier_gram.shape
    chips = n // 2
    k_half = k_out // 2
    k_chunk = k_half // chips
    per_group = n // groups
    any_spec = pl.BlockSpec(memory_space=pl.ANY)
    vmem_spec = pl.BlockSpec(memory_space=pltpu.VMEM)
    f32, bf16 = jnp.float32, jnp.bfloat16
    dma = pltpu.SemaphoreType.DMA

    left, right, held = pl.pallas_call(
        functools.partial(feature_kernel, n, groups, count, scale),
        out_shape=(
            pltpu.VMEM((3 * examples, row_width), bf16),
            pltpu.VMEM((3 * examples, col_width), bf16),
            pltpu.VMEM((row_width, col_width), f32),
        ),
        in_specs=[any_spec] * 5,
        out_specs=(vmem_spec, vmem_spec, vmem_spec),
        scratch_shapes=[
            pltpu.VMEM((tokens, width), bf16),
            pltpu.VMEM((tokens, width), bf16),
            pltpu.VMEM((draws, width, k_in), bf16),
            pltpu.VMEM((draws, k_out, width), bf16),
            pltpu.VMEM((tokens, draws * k_in), bf16),
            pltpu.VMEM((draws * k_out, tokens), bf16),
            pltpu.VMEM((k_half, count, k_in), f32),
            pltpu.VMEM((k_half, count, k_in), f32),
            pltpu.VMEM((k_half, count, k_in), f32),
            pltpu.VMEM((chips - 1, k_chunk, count, k_in), f32),
            pltpu.VMEM((k_chunk, count, k_in), f32),
            pltpu.VMEM((per_group, groups, k_chunk, count, k_in), f32),
            pltpu.VMEM((groups, k_chunk, count, k_in), f32),
            dma((2 * DEPTHS * (HALVES + 1),)),
            dma((2,)),
            dma((chips - 1,)),
            dma((chips - 1,)),
            dma((chips,)),
            dma((per_group, groups)),
            dma((per_group, groups)),
            dma((groups,)),
            dma((groups,)),
            dma,
        ],
        compiler_params=pltpu.CompilerParams(
            collective_id=0, has_side_effects=True, vmem_limit_bytes=52 << 20
        ),
        name="features",
    )(
        activations.reshape(tokens, width),
        out_grads.reshape(tokens, width),
        proj_in[0],
        proj_out[0],
        earlier_gram,
    )
    tiles = 8
    return pl.pallas_call(
        functools.partial(gram_kernel, tiles),
        out_shape=jax.ShapeDtypeStruct((row_width, col_width), f32),
        in_specs=[vmem_spec, vmem_spec, vmem_spec],
        out_specs=any_spec,
        scratch_shapes=[pltpu.VMEM((row_width, col_width), f32), dma((tiles,))],
        compiler_params=pltpu.CompilerParams(vmem_limit_bytes=28 << 20),
        name="gram",
    )(left, right, held)


def solution(mesh):
    return jax.shard_map(
        per_device,
        mesh=mesh,
        in_specs=(
            P("section", "dp", None, None),
            P("section", "dp", None, None),
            P("section", None, None, None),
            P("section", None, None, None),
            P("section", "dp"),
        ),
        out_specs=P("section", "dp"),
        check_vma=False,
    )
```

profile of v0, /device:TPU:0, one launch (start us, length us, event | category | flops | bytes accessed | tf_op | source)
XLA Modules:
  0.0 28.4 jit_solution(11641533325137412328)
XLA Ops:
  0.0 24.7 %features.1 = (bf16[48,512]{1,0:T(8,128)(2,1)S(1)}, bf16[48,4096]{1,0:T(8,128)(2,1)S(1)}, f32[512,4096]{1,0:T(8,128)S(1)}) custom-call(bf16[512,4096]{1,0:T(8,128)(2,1)} %bitcast.4, bf16[512,4096]{1,0:T(8,128)(2,1)} %bitcast.5, bf16[2,4096,128]{2,1,0:T(8,128)(2,1)} %bitcast.6, bf16[2,64,4096]{2,1,0:T(8,128)(2,1)} %bitcast.7, f32[512,4096]{1,0:T(8,128)} %earlier.1), custom_call_target="tpu_custom_call" | custom-call | tf_op jit(solution)/shard_map/features/pallas_call | solution.py:303
  24.7 3.7 %gram.1 = f32[512,4096]{1,0:T(8,128)} custom-call(bf16[48,512]{1,0:T(8,128)(2,1)S(1)} %get-tuple-element.8.left, bf16[48,4096]{1,0:T(8,128)(2,1)S(1)} %get-tuple-element.9.right, f32[512,4096]{1,0:T(8,128)S(1)} %get-tuple-element.10.earlier), custom_call_target="tpu_custom_call" | custom-call | tf_op jit(solution)/shard_map/gram/pallas_call | solution.py:349
where the time goes:
time: 28.5 us; the launch traced here: 28.4 us
  Pallas kernels  28.4 us (100%)
    pallas_call x1, Pallas kernels, per_device(): pl.pallas_call(functools.partial(feature_kernel, n, groups, count, scale)...  24.7 us
    pallas_call x1, Pallas kernels, per_device(): pl.pallas_call(functools.partial(gram_kernel, tiles), out_shape=jax.Shape...  3.69 us

commit v1 on v0

--- a/solution.py
+++ b/solution.py
@@ -10,9 +10,9 @@
 
 MESH = pl.DeviceIdType.MESH
 LANES = 128
-HALVES = 2
-DEPTHS = 1
-WINDOW = 4
+SPLITS = 1
+DEPTHS = (8,)
+FIRST = 8
 
 
 def split(x):
@@ -25,8 +25,8 @@
     n, groups, count, scale,
     act, grad, p_in, p_out, earlier,
     left, right, held,
-    act_v, grad_v, in_v, out_v, low_in, low_out,
-    mine, theirs, arrived, pieces, own, cols, row,
+    act_v, grad_v, in_v, out_v,
+    phi, arrived, pieces, own, cols, row,
     load_sem, pair_sem, send_sem, recv_sem,
     col_send, col_recv, fwd_send, row_send, row_recv, held_sem,
 ):
@@ -41,83 +41,66 @@
     k_out = p_out.shape[1]
     tokens = act.shape[0]
     length = tokens // count
-    rows = tokens // HALVES
-    depth = width // DEPTHS
-
-    loads = {}
-    slot = 0
-    for h in range(HALVES):
-        for c in range(DEPTHS):
+
+    copies = {}
+
+    def fetch(key, src, dst):
+        copies[key] = pltpu.make_async_copy(src, dst, load_sem.at[len(copies)])
+
+    bounds = [count * i // SPLITS for i in range(SPLITS + 1)]
+    for h in range(SPLITS):
+        rs = pl.ds(bounds[h] * length, (bounds[h + 1] - bounds[h]) * length)
+        pieces_of = DEPTHS[h]
+        depth = width // pieces_of
+        for c in range(pieces_of):
             cs = pl.ds(c * depth, depth)
-            rs = pl.ds(h * rows, rows)
-            wanted = []
             if h == 0:
-                wanted.append(("p_in", p_in.at[:, cs], in_v.at[:, cs]))
-            wanted.append(("act", act.at[rs, cs], act_v.at[rs, cs]))
-            if h == 0:
-                wanted.append(("p_out", p_out.at[:, :, cs], out_v.at[:, :, cs]))
-            wanted.append(("grad", grad.at[rs, cs], grad_v.at[rs, cs]))
-            for name, src, dst in wanted:
-                copy = pltpu.make_async_copy(src, dst, load_sem.at[slot])
-                loads[name, h, c] = copy
-                slot += 1
-    queue = list(loads.values())
-
-    def take(copy):
-        copy.wait()
-        if queue:
-            queue.pop(0).start()
-
-    for _ in range(WINDOW):
-        queue.pop(0).start()
-
+                fetch(("p_in", c), p_in.at[:, cs], in_v.at[:, cs])
+                fetch(("p_out", c), p_out.at[:, :, cs], out_v.at[:, :, cs])
+            fetch(("act", h, c), act.at[rs, cs], act_v.at[rs, cs])
+            fetch(("grad", h, c), grad.at[rs, cs], grad_v.at[rs, cs])
+    queue = list(copies.values())
+    for copy in queue[:FIRST]:
+        copy.start()
     barrier = pltpu.get_barrier_semaphore()
     for g in range(groups):
         for i in range(n):
-            if g or i:
-                peer = {"section": (s + i) % n, "dp": (d + g) % groups}
-                pl.semaphore_signal(barrier, inc=1, device_id=peer, device_id_type=MESH)
-
-    for h in range(HALVES):
-        rs = slice(h * rows, (h + 1) * rows)
+            pl.semaphore_signal(barrier, inc=1, device_id={"section": i, "dp": g}, device_id_type=MESH)
+    for copy in queue[FIRST:]:
+        copy.start()
+
+    k_half = k_out // 2
+    for h in range(SPLITS):
+        lo, hi = bounds[h], bounds[h + 1]
+        rs = slice(lo * length, hi * length)
+        depth = width // DEPTHS[h]
         total_in = total_out = None
-        for c in range(DEPTHS):
+        for c in range(DEPTHS[h]):
             cs = slice(c * depth, (c + 1) * depth)
             if h == 0:
-                take(loads["p_in", h, c])
-            take(loads["act", h, c])
+                copies["p_in", c].wait()
+                copies["p_out", c].wait()
+            copies["act", h, c].wait()
+            copies["grad", h, c].wait()
             weights = jnp.concatenate([in_v[p, cs, :] for p in range(draws)], axis=1)
-            term = jnp.dot(act_v[rs, cs], weights, preferred_element_type=jnp.float32)
-            total_in = term if total_in is None else total_in + term
-            if h == 0:
-                take(loads["p_out", h, c])
-            take(loads["grad", h, c])
+            term_in = jnp.dot(act_v[rs, cs], weights, preferred_element_type=jnp.float32)
             weights = out_v[:, :, cs].reshape(draws * k_out, depth)
-            term = lax.dot_general(
+            term_out = lax.dot_general(
                 grad_v[rs, cs], weights, (((1,), (1,)), ((), ())), preferred_element_type=jnp.float32
             )
-            total_out = term if total_out is None else total_out + term
-        if h == HALVES - 1:
+            total_in = term_in if total_in is None else total_in + term_in
+            total_out = term_out if total_out is None else total_out + term_out
+        if h == SPLITS - 1:
             hold = pltpu.make_async_copy(earlier, held, held_sem)
             hold.start()
-        low_in[rs, :] = total_in.astype(jnp.bfloat16)
-        low_out[:, rs] = total_out.T.astype(jnp.bfloat16)
-
-    k_half = k_out // 2
-
-    def terms(which, into):
-        for e in range(count):
-            ts = slice(e * length, (e + 1) * length)
-            value = None
-            for p in range(draws):
-                start = pl.multiple_of(p * k_out + which * k_half, k_half)
-                term = jnp.dot(
-                    low_out[pl.ds(start, k_half), ts],
-                    low_in[ts, p * k_in:(p + 1) * k_in],
-                    preferred_element_type=jnp.float32,
-                )
-                value = term if value is None else value + term
-            into[:, e, :] = value
+        in_part = total_in.astype(jnp.bfloat16)
+        for e in range(lo, hi):
+            ts = slice((e - lo) * length, (e - lo + 1) * length)
+            lhs = jnp.concatenate([total_out[ts, p * k_out:(p + 1) * k_out] for p in range(draws)], axis=0)
+            rhs = jnp.concatenate([in_part[ts, p * k_in:(p + 1) * k_in] for p in range(draws)], axis=0)
+            phi[pl.ds(e, k_out, stride=count), :] = jnp.dot(
+                lhs.T.astype(jnp.bfloat16), rhs, preferred_element_type=jnp.float32
+            )
 
     def remote(src, dst, ssem, rsem, section, dp):
         return pltpu.make_async_remote_copy(
@@ -125,11 +108,12 @@
             device_id={"section": section, "dp": dp}, device_id_type=MESH,
         )
 
-    terms(1 - core, theirs)
-    pl.semaphore_wait(barrier, n * groups - 1)
+    half_rows = k_half * count
+    pl.semaphore_wait(barrier, n * groups)
+    theirs = phi.at[pl.ds(pl.multiple_of((1 - core) * half_rows, half_rows), half_rows)]
+    mine = phi.at[pl.ds(pl.multiple_of(core * half_rows, half_rows), half_rows)]
     swap = remote(theirs, arrived, pair_sem.at[0], pair_sem.at[1], partner, d)
     swap.start()
-    terms(core, mine)
     swap.wait_recv()
 
     def across(c, i):
@@ -141,16 +125,17 @@
         return c
 
     k_chunk = k_half // chips
+    rows = k_chunk * count
     sends = []
     for i in range(chips - 1, 0, -1):
         to = across(chip, i)
-        ks = pl.ds(to * k_chunk, k_chunk)
-        mine[ks] = mine[ks] + arrived[ks]
+        ks = pl.ds(pl.multiple_of(to * rows, rows), rows)
+        mine[ks, :] = mine[ks, :] + arrived[ks, :]
         copy = remote(mine.at[ks], pieces.at[i - 1], send_sem.at[i - 1], recv_sem.at[i - 1], 2 * to + core, d)
         copy.start()
         sends.append(copy)
-    ks = pl.ds(chip * k_chunk, k_chunk)
-    total = mine[ks] + arrived[ks]
+    ks = pl.ds(pl.multiple_of(chip * rows, rows), rows)
+    total = mine[ks, :] + arrived[ks, :]
     for i in range(1, chips):
         sends[chips - 1 - i].wait_recv()
         total = total + pieces[i - 1]
@@ -216,7 +201,7 @@
                 forward(j, g).start()
 
         for k in range(k_chunk):
-            hi, lo = split(jnp.concatenate([cols[j, g, k] for g in range(groups)], axis=0))
+            hi, lo = split(jnp.concatenate([cols[j, g, k * count:(k + 1) * count] for g in range(groups)], axis=0))
             at = pl.multiple_of((j * k_chunk + k) * LANES, LANES)
             right[:, pl.ds(at, LANES)] = jnp.concatenate([hi, hi, lo], axis=0)
 
@@ -231,7 +216,7 @@
         row[...] = cols[s % per_group]
 
     for k in range(k_chunk):
-        hi, lo = split(jnp.concatenate([row[g, k] for g in range(groups)], axis=0) * scale)
+        hi, lo = split(jnp.concatenate([row[g, k * count:(k + 1) * count] for g in range(groups)], axis=0) * scale)
         left[:, k * LANES:(k + 1) * LANES] = jnp.concatenate([hi, lo, hi], axis=0)
 
     hold.wait()
@@ -314,16 +299,13 @@
             pltpu.VMEM((tokens, width), bf16),
             pltpu.VMEM((draws, width, k_in), bf16),
             pltpu.VMEM((draws, k_out, width), bf16),
-            pltpu.VMEM((tokens, draws * k_in), bf16),
-            pltpu.VMEM((draws * k_out, tokens), bf16),
-            pltpu.VMEM((k_half, count, k_in), f32),
-            pltpu.VMEM((k_half, count, k_in), f32),
-            pltpu.VMEM((k_half, count, k_in), f32),
-            pltpu.VMEM((chips - 1, k_chunk, count, k_in), f32),
-            pltpu.VMEM((k_chunk, count, k_in), f32),
-            pltpu.VMEM((per_group, groups, k_chunk, count, k_in), f32),
-            pltpu.VMEM((groups, k_chunk, count, k_in), f32),
-            dma((2 * DEPTHS * (HALVES + 1),)),
+            pltpu.VMEM((k_out * count, k_in), f32),
+            pltpu.VMEM((k_half * count, k_in), f32),
+            pltpu.VMEM((chips - 1, k_chunk * count, k_in), f32),
+            pltpu.VMEM((k_chunk * count, k_in), f32),
+            pltpu.VMEM((per_group, groups, k_chunk * count, k_in), f32),
+            pltpu.VMEM((groups, k_chunk * count, k_in), f32),
+            dma((2 * (DEPTHS[0] + sum(DEPTHS)),)),
             dma((2,)),
             dma((chips - 1,)),
             dma((chips - 1,)),

time: 28.5 us -> 26.4 us (0.926)
  Pallas kernels: 28.4 us -> 26.2 us
    pallas_call x1, Pallas kernels: 24.7 us -> 22.5 us  [per_device(): pl.pallas_call(functools.partial(feature_kernel, n, groups, count, scale)...]
where the time goes in v1:
time: 26.4 us; the launch traced here: 26.2 us
  Pallas kernels  26.2 us (99%)
    pallas_call x1, Pallas kernels, per_device(): pl.pallas_call(functools.partial(feature_kernel, n, groups, count, scale)...  22.5 us
    pallas_call x1, Pallas kernels, per_device(): pl.pallas_call(functools.partial(gram_kernel, tiles), out_shape=jax.Shape...  3.68 us

profile of v1, /device:TPU:0, one launch (start us, length us, event | category | flops | bytes accessed | tf_op | source)
XLA Modules:
  0.0 26.2 jit_solution(1752266174623309491)
XLA Ops:
  0.0 22.5 %features.1 = (bf16[48,512]{1,0:T(8,128)(2,1)S(1)}, bf16[48,4096]{1,0:T(8,128)(2,1)S(1)}, f32[512,4096]{1,0:T(8,128)S(1)}) custom-call(bf16[512,4096]{1,0:T(8,128)(2,1)} %bitcast.4, bf16[512,4096]{1,0:T(8,128)(2,1)} %bitcast.5, bf16[2,4096,128]{2,1,0:T(8,128)(2,1)} %bitcast.6, bf16[2,64,4096]{2,1,0:T(8,128)(2,1)} %bitcast.7, f32[512,4096]{1,0:T(8,128)} %earlier.1), custom_call_target="tpu_custom_call" | custom-call | tf_op jit(solution)/shard_map/features/pallas_call | solution.py:288
  22.5 3.7 %gram.1 = f32[512,4096]{1,0:T(8,128)} custom-call(bf16[48,512]{1,0:T(8,128)(2,1)S(1)} %get-tuple-element.8.left, bf16[48,4096]{1,0:T(8,128)(2,1)S(1)} %get-tuple-element.9.right, f32[512,4096]{1,0:T(8,128)S(1)} %get-tuple-element.10.earlier), custom_call_target="tpu_custom_call" | custom-call | tf_op jit(solution)/shard_map/gram/pallas_call | solution.py:331

commit v2 on v1

v2 whole, which is shorter than its diff:
```python
import functools
import math

import jax
import jax.numpy as jnp
from jax import lax
from jax.experimental import pallas as pl
from jax.experimental.pallas import tpu as pltpu
from jax.sharding import PartitionSpec as P

MESH = pl.DeviceIdType.MESH
LANES = 128
PIECES = 8
FIRST = 2


def split(x):
    hi = x.astype(jnp.bfloat16)
    lo = (x - hi.astype(jnp.float32)).astype(jnp.bfloat16)
    return hi, lo


def feature_kernel(
    n, groups, count, scale,
    act, grad, p_in, p_out, earlier,
    left, right, held,
    act_v, grad_v, in_v, out_v,
    phi, arrived, pieces, own, cols, row,
    load_sem, pair_sem, send_sem, recv_sem, col_recv, row_send, row_recv, held_sem,
):
    s = lax.axis_index("section")
    d = lax.axis_index("dp")
    chips = n // 2
    core = s % 2
    chip = s // 2
    partner = s + 1 - 2 * core

    draws, width, k_in = p_in.shape
    k_out = p_out.shape[1]
    tokens = act.shape[0]
    length = tokens // count

    depth = width // PIECES
    loads = []
    for c in range(PIECES):
        cs = pl.ds(c * depth, depth)
        sem = load_sem.at[c]
        loads.append([
            pltpu.make_async_copy(p_in.at[:, cs], in_v.at[:, cs], sem),
            pltpu.make_async_copy(p_out.at[:, :, cs], out_v.at[:, :, cs], sem),
            pltpu.make_async_copy(act.at[:, cs], act_v.at[:, cs], sem),
            pltpu.make_async_copy(grad.at[:, cs], grad_v.at[:, cs], sem),
        ])

    def start(some):
        for piece in some:
            for copy in piece:
                copy.start()

    start(loads[:FIRST])
    barrier = pltpu.get_barrier_semaphore()
    for g in range(groups):
        for i in range(n):
            pl.semaphore_signal(barrier, inc=1, device_id={"section": i, "dp": g}, device_id_type=MESH)
    start(loads[FIRST:])

    piece_rows = depth * (draws * (k_in + k_out) + 2 * tokens) // width
    total_in = total_out = None
    for c in range(PIECES):
        cs = slice(c * depth, (c + 1) * depth)
        pltpu.make_async_copy(act.at[pl.ds(0, piece_rows)], act_v.at[pl.ds(0, piece_rows)], load_sem.at[c]).wait()
        weights = jnp.concatenate([in_v[p, cs, :] for p in range(draws)], axis=1)
        term_in = jnp.dot(act_v[:, cs], weights, preferred_element_type=jnp.float32)
        weights = out_v[:, :, cs].reshape(draws * k_out, depth)
        term_out = lax.dot_general(
            grad_v[:, cs], weights, (((1,), (1,)), ((), ())), preferred_element_type=jnp.float32
        )
        total_in = term_in if total_in is None else total_in + term_in
        total_out = term_out if total_out is None else total_out + term_out
    low_in = total_in.astype(jnp.bfloat16)
    k_half = k_out // 2
    half_rows = k_half * count
    for e in range(count):
        ts = slice(e * length, (e + 1) * length)
        lhs = jnp.concatenate([total_out[ts, p * k_out:(p + 1) * k_out] for p in range(draws)], axis=0)
        rhs = jnp.concatenate([low_in[ts, p * k_in:(p + 1) * k_in] for p in range(draws)], axis=0)
        phi[pl.ds(e, k_out, stride=count), :] = jnp.dot(
            lhs.T.astype(jnp.bfloat16), rhs, preferred_element_type=jnp.float32
        )
    def remote(src, dst, ssem, rsem, section, dp):
        return pltpu.make_async_remote_copy(
            src_ref=src, dst_ref=dst, send_sem=ssem, recv_sem=rsem,
            device_id={"section": section, "dp": dp}, device_id_type=MESH,
        )

    pl.semaphore_wait(barrier, n * groups)
    theirs = phi.at[pl.ds(pl.multiple_of((1 - core) * half_rows, half_rows), half_rows)]
    mine = phi.at[pl.ds(pl.multiple_of(core * half_rows, half_rows), half_rows)]
    swap = remote(theirs, arrived, pair_sem.at[0], pair_sem.at[1], partner, d)
    swap.start()
    swap.wait_recv()

    def across(c, i):
        bit = 1
        while bit < chips:
            if i & bit:
                c = c + bit * (1 - 2 * ((c // bit) % 2))
            bit *= 2
        return c

    k_chunk = k_half // chips
    rows = k_chunk * count
    for i in range(chips - 1, 0, -1):
        to = across(chip, i)
        ks = pl.ds(pl.multiple_of(to * rows, rows), rows)
        mine[ks, :] = mine[ks, :] + arrived[ks, :]
        remote(mine.at[ks], pieces.at[i - 1], send_sem.at[0], recv_sem.at[0], 2 * to + core, d).start()
    hold = pltpu.make_async_copy(earlier, held, held_sem)
    hold.start()
    ks = pl.ds(pl.multiple_of(chip * rows, rows), rows)
    total = mine[ks, :] + arrived[ks, :]
    exchange = remote(pieces, pieces, send_sem.at[0], recv_sem.at[0], partner, d)
    exchange.wait_recv()
    for i in range(1, chips):
        total = total + pieces[i - 1]
    own[...] = total

    per_group = n // groups
    q = core * chips + chip
    own_slot = q % per_group
    home = q // per_group
    at_home = home == d

    def col_copy(to):
        return remote(own, cols.at[own_slot, d], send_sem.at[1], col_recv.at[own_slot], 2 * to + core, home)

    for i in range(chips - 1):
        col_copy(jnp.where(chip <= i, i + 1, i)).start()
    cross = jnp.logical_not(at_home)

    @pl.when(at_home)
    def _():
        remote(own, cols.at[own_slot, d], send_sem.at[1], col_recv.at[own_slot], partner, d).start()
        cols[own_slot, d] = own[...]

    @pl.when(cross)
    def _():
        col_copy(chip).start()

    row_here = jnp.logical_and(q == s, home != d)
    for g in range(groups):
        here = jnp.logical_and(q == s, d == g)

        @pl.when(jnp.logical_and(home != g, jnp.logical_not(here)))
        def _():
            remote(own, row.at[d], row_send.at[g], row_recv.at[d], q, g).start()

        @pl.when(jnp.logical_and(home != g, here))
        def _():
            row[d] = own[...]

    def forward(j, lo, size, sem):
        ref = cols.at[j, pl.ds(lo, size)]
        return remote(ref, ref, send_sem.at[sem], col_recv.at[j], partner, d)

    passes = d * per_group // chips == core
    for i in range(per_group):
        j = across(chip, i) % per_group
        mixed = d * per_group + j == q

        @pl.when(jnp.logical_not(mixed))
        def _():
            forward(j, 0, groups, 2).wait_recv()

            @pl.when(passes)
            def _():
                forward(j, 0, groups, 2).start()

        @pl.when(mixed)
        def _():
            forward(j, 0, groups - 1, 3).wait_recv()
            for g in range(groups):

                @pl.when(d != g)
                def _():
                    forward(j, g, 1, 3).start()

        for k in range(k_chunk):
            hi, lo = split(jnp.concatenate([cols[j, g, k * count:(k + 1) * count] for g in range(groups)], axis=0))
            at = pl.multiple_of((j * k_chunk + k) * LANES, LANES)
            right[:, pl.ds(at, LANES)] = jnp.concatenate([hi, hi, lo], axis=0)

    for g in range(groups):

        @pl.when(jnp.logical_and(s // per_group != d, jnp.logical_or(q != s, d != g)))
        def _():
            remote(own, row.at[g], row_send.at[g], row_recv.at[g], q, d).wait_recv()

    @pl.when(s // per_group == d)
    def _():
        row[...] = cols[s % per_group]

    for k in range(k_chunk):
        hi, lo = split(jnp.concatenate([row[g, k * count:(k + 1) * count] for g in range(groups)], axis=0) * scale)
        left[:, k * LANES:(k + 1) * LANES] = jnp.concatenate([hi, lo, hi], axis=0)

    hold.wait()
    swap.wait_send()
    exchange.wait_send()
    remote(arrived, arrived, send_sem.at[1], recv_sem.at[0], partner, d).wait_send()
    for g in range(groups):

        @pl.when(jnp.logical_and(home != g, jnp.logical_or(q != s, d != g)))
        def _():
            remote(own, row.at[d], row_send.at[g], row_recv.at[d], q, g).wait_send()

    def forwarded(count, sem):
        ref = cols.at[pl.ds(0, count)]
        remote(ref, ref, send_sem.at[sem], recv_sem.at[0], partner, d).wait_send()

    @pl.when(at_home)
    def _():
        forwarded(per_group - 1, 2)
        forward(0, 0, groups - 1, 3).wait_send()

    @pl.when(jnp.logical_and(passes, cross))
    def _():
        forwarded(per_group, 2)


def gram_kernel(tiles, left, right, earlier, out, tile_v, sem):
    columns = right.shape[1] // tiles
    lhs = left[...].T
    copies = []
    for i in range(tiles):
        cs = slice(i * columns, (i + 1) * columns)
        tile_v[:, cs] = earlier[:, cs] + jnp.dot(lhs, right[:, cs], preferred_element_type=jnp.float32)
        copy = pltpu.make_async_copy(
            tile_v.at[:, pl.ds(i * columns, columns)], out.at[:, pl.ds(i * columns, columns)], sem.at[i]
        )
        copy.start()
        copies.append(copy)
    for copy in copies:
        copy.wait()


def per_device(activations, out_grads, proj_in, proj_out, earlier_gram):
    n = lax.axis_size("section")
    groups = lax.axis_size("dp")
    _, count, length, width = activations.shape
    _, draws, _, k_in = proj_in.shape
    k_out = proj_out.shape[2]
    tokens = count * length
    examples = count * groups
    scale = 1.0 / (length * n * draws) / examples
    row_width, col_width = earlier_gram.shape
    chips = n // 2
    k_half = k_out // 2
    k_chunk = k_half // chips
    per_group = n // groups
    any_spec = pl.BlockSpec(memory_space=pl.ANY)
    vmem_spec = pl.BlockSpec(memory_space=pltpu.VMEM)
    f32, bf16 = jnp.float32, jnp.bfloat16
    dma = pltpu.SemaphoreType.DMA

    left, right, held = pl.pallas_call(
        functools.partial(feature_kernel, n, groups, count, scale),
        out_shape=(
            pltpu.VMEM((3 * examples, row_width), bf16),
            pltpu.VMEM((3 * examples, col_width), bf16),
            pltpu.VMEM((row_width, col_width), f32),
        ),
        in_specs=[any_spec] * 5,
        out_specs=(vmem_spec, vmem_spec, vmem_spec),
        scratch_shapes=[
            pltpu.VMEM((tokens, width), bf16),
            pltpu.VMEM((tokens, width), bf16),
            pltpu.VMEM((draws, width, k_in), bf16),
            pltpu.VMEM((draws, k_out, width), bf16),
            pltpu.VMEM((k_out * count, k_in), f32),
            pltpu.VMEM((k_half * count, k_in), f32),
            pltpu.VMEM((chips - 1, k_chunk * count, k_in), f32),
            pltpu.VMEM((k_chunk * count, k_in), f32),
            pltpu.VMEM((per_group, groups, k_chunk * count, k_in), f32),
            pltpu.VMEM((groups, k_chunk * count, k_in), f32),
            dma((PIECES,)),
            dma((2,)),
            dma((4,)),
            dma((1,)),
            dma((per_group,)),
            dma((groups,)),
            dma((groups,)),
            dma,
        ],
        compiler_params=pltpu.CompilerParams(
            collective_id=0, has_side_effects=True, vmem_limit_bytes=52 << 20
        ),
        name="features",
    )(
        activations.reshape(tokens, width),
        out_grads.reshape(tokens, width),
        proj_in[0],
        proj_out[0],
        earlier_gram,
    )
    tiles = 8
    return pl.pallas_call(
        functools.partial(gram_kernel, tiles),
        out_shape=jax.ShapeDtypeStruct((row_width, col_width), f32),
        in_specs=[vmem_spec, vmem_spec, vmem_spec],
        out_specs=any_spec,
        scratch_shapes=[pltpu.VMEM((row_width, col_width), f32), dma((tiles,))],
        compiler_params=pltpu.CompilerParams(vmem_limit_bytes=28 << 20),
        name="gram",
    )(left, right, held)


def solution(mesh):
    return jax.shard_map(
        per_device,
        mesh=mesh,
        in_specs=(
            P("section", "dp", None, None),
            P("section", "dp", None, None),
            P("section", None, None, None),
            P("section", None, None, None),
            P("section", "dp"),
        ),
        out_specs=P("section", "dp"),
        check_vma=False,
    )
```

time: 26.4 us -> 25.2 us (0.955)
  Pallas kernels: 26.2 us -> 25 us
    pallas_call x1, Pallas kernels: 22.5 us -> 21.3 us  [per_device(): pl.pallas_call(functools.partial(feature_kernel, n, groups, count, scale)...]
where the time goes in v2:
time: 25.2 us; the launch traced here: 25 us
  Pallas kernels  25 us (99%)
    pallas_call x1, Pallas kernels, per_device(): pl.pallas_call(functools.partial(feature_kernel, n, groups, count, scale)...  21.3 us
    pallas_call x1, Pallas kernels, per_device(): pl.pallas_call(functools.partial(gram_kernel, tiles), out_shape=jax.Shape...  3.68 us

profile of v2, /device:TPU:0, one launch (start us, length us, event | category | flops | bytes accessed | tf_op | source)
XLA Modules:
  0.0 25.0 jit_solution(12734165403936964727)
XLA Ops:
  0.0 21.3 %features.1 = (bf16[48,512]{1,0:T(8,128)(2,1)S(1)}, bf16[48,4096]{1,0:T(8,128)(2,1)S(1)}, f32[512,4096]{1,0:T(8,128)S(1)}) custom-call(bf16[512,4096]{1,0:T(8,128)(2,1)} %bitcast.4, bf16[512,4096]{1,0:T(8,128)(2,1)} %bitcast.5, bf16[2,4096,128]{2,1,0:T(8,128)(2,1)} %bitcast.6, bf16[2,64,4096]{2,1,0:T(8,128)(2,1)} %bitcast.7, f32[512,4096]{1,0:T(8,128)} %earlier.1), custom_call_target="tpu_custom_call" | custom-call | tf_op jit(solution)/shard_map/features/pallas_call | solution.py:266
  21.3 3.7 %gram.1 = f32[512,4096]{1,0:T(8,128)} custom-call(bf16[48,512]{1,0:T(8,128)(2,1)S(1)} %get-tuple-element.8.left, bf16[48,4096]{1,0:T(8,128)(2,1)S(1)} %get-tuple-element.9.right, f32[512,4096]{1,0:T(8,128)S(1)} %get-tuple-element.10.earlier), custom_call_target="tpu_custom_call" | custom-call | tf_op jit(solution)/shard_map/gram/pallas_call | solution.py:307

commit v3 on v2

--- a/solution.py
+++ b/solution.py
@@ -10,7 +10,7 @@
 
 MESH = pl.DeviceIdType.MESH
 LANES = 128
-PIECES = 8
+PIECES = (3, 3, 3, 3, 2, 1, 1)
 FIRST = 2
 
 
@@ -40,10 +40,14 @@
     tokens = act.shape[0]
     length = tokens // count
 
-    depth = width // PIECES
-    loads = []
-    for c in range(PIECES):
-        cs = pl.ds(c * depth, depth)
+    loads, spans, row_counts = [], [], []
+    at = 0
+    for c, part in enumerate(PIECES):
+        depth = width * part // sum(PIECES)
+        spans.append(slice(at, at + depth))
+        row_counts.append(depth * (draws * (k_in + k_out) + 2 * tokens) // width)
+        cs = pl.ds(at, depth)
+        at += depth
         sem = load_sem.at[c]
         loads.append([
             pltpu.make_async_copy(p_in.at[:, cs], in_v.at[:, cs], sem),
@@ -64,14 +68,12 @@
             pl.semaphore_signal(barrier, inc=1, device_id={"section": i, "dp": g}, device_id_type=MESH)
     start(loads[FIRST:])
 
-    piece_rows = depth * (draws * (k_in + k_out) + 2 * tokens) // width
     total_in = total_out = None
-    for c in range(PIECES):
-        cs = slice(c * depth, (c + 1) * depth)
+    for c, (cs, piece_rows) in enumerate(zip(spans, row_counts)):
         pltpu.make_async_copy(act.at[pl.ds(0, piece_rows)], act_v.at[pl.ds(0, piece_rows)], load_sem.at[c]).wait()
         weights = jnp.concatenate([in_v[p, cs, :] for p in range(draws)], axis=1)
         term_in = jnp.dot(act_v[:, cs], weights, preferred_element_type=jnp.float32)
-        weights = out_v[:, :, cs].reshape(draws * k_out, depth)
+        weights = out_v[:, :, cs].reshape(draws * k_out, cs.stop - cs.start)
         term_out = lax.dot_general(
             grad_v[:, cs], weights, (((1,), (1,)), ((), ())), preferred_element_type=jnp.float32
         )
@@ -110,7 +112,8 @@
 
     k_chunk = k_half // chips
     rows = k_chunk * count
-    for i in range(chips - 1, 0, -1):
+    turns = [2 * (m ^ m // 2) + b for m in range(1, chips // 2) for b in (0, 1)] + [1]
+    for i in turns:
         to = across(chip, i)
         ks = pl.ds(pl.multiple_of(to * rows, rows), rows)
         mine[ks, :] = mine[ks, :] + arrived[ks, :]
@@ -229,19 +232,18 @@
 
 
 def gram_kernel(tiles, left, right, earlier, out, tile_v, sem):
-    columns = right.shape[1] // tiles
+    height = earlier.shape[0] // tiles
     lhs = left[...].T
     copies = []
     for i in range(tiles):
-        cs = slice(i * columns, (i + 1) * columns)
-        tile_v[:, cs] = earlier[:, cs] + jnp.dot(lhs, right[:, cs], preferred_element_type=jnp.float32)
+        rs = slice(i * height, (i + 1) * height)
+        tile_v[rs, :] = earlier[rs, :] + jnp.dot(lhs[rs], right[...], preferred_element_type=jnp.float32)
         copy = pltpu.make_async_copy(
-            tile_v.at[:, pl.ds(i * columns, columns)], out.at[:, pl.ds(i * columns, columns)], sem.at[i]
+            tile_v.at[pl.ds(i * height, height)], out.at[pl.ds(i * height, height)], sem.at[0]
         )
         copy.start()
         copies.append(copy)
-    for copy in copies:
-        copy.wait()
+    pltpu.make_async_copy(tile_v, out, sem.at[0]).wait()
 
 
 def per_device(activations, out_grads, proj_in, proj_out, earlier_gram):
@@ -283,7 +285,7 @@
             pltpu.VMEM((k_chunk * count, k_in), f32),
             pltpu.VMEM((per_group, groups, k_chunk * count, k_in), f32),
             pltpu.VMEM((groups, k_chunk * count, k_in), f32),
-            dma((PIECES,)),
+            dma((len(PIECES),)),
             dma((2,)),
             dma((4,)),
             dma((1,)),
@@ -303,13 +305,13 @@
         proj_out[0],
         earlier_gram,
     )
-    tiles = 8
+    tiles = 16
     return pl.pallas_call(
         functools.partial(gram_kernel, tiles),
         out_shape=jax.ShapeDtypeStruct((row_width, col_width), f32),
         in_specs=[vmem_spec, vmem_spec, vmem_spec],
         out_specs=any_spec,
-        scratch_shapes=[pltpu.VMEM((row_width, col_width), f32), dma((tiles,))],
+        scratch_shapes=[pltpu.VMEM((row_width, col_width), f32), dma((1,))],
         compiler_params=pltpu.CompilerParams(vmem_limit_bytes=28 << 20),
         name="gram",
     )(left, right, held)

time: 25.2 us -> 24.2 us (0.960)
  Pallas kernels: 25 us -> 24 us
    pallas_call x1, Pallas kernels: 21.3 us -> 20.5 us  [per_device(): pl.pallas_call(functools.partial(feature_kernel, n, groups, count, scale)...]
where the time goes in v3:
time: 24.2 us; the launch traced here: 24.1 us
  Pallas kernels  24 us (99%)
    pallas_call x1, Pallas kernels, per_device(): pl.pallas_call(functools.partial(feature_kernel, n, groups, count, scale)...  20.5 us
    pallas_call x1, Pallas kernels, per_device(): pl.pallas_call(functools.partial(gram_kernel, tiles), out_shape=jax.Shape...  3.54 us

profile of v3, /device:TPU:0, one launch (start us, length us, event | category | flops | bytes accessed | tf_op | source)
XLA Modules:
  0.0 24.1 jit_solution(7141869371046839911)
XLA Ops:
  0.0 20.5 %features.1 = (bf16[48,512]{1,0:T(8,128)(2,1)S(1)}, bf16[48,4096]{1,0:T(8,128)(2,1)S(1)}, f32[512,4096]{1,0:T(8,128)S(1)}) custom-call(bf16[512,4096]{1,0:T(8,128)(2,1)} %bitcast.4, bf16[512,4096]{1,0:T(8,128)(2,1)} %bitcast.5, bf16[2,4096,128]{2,1,0:T(8,128)(2,1)} %bitcast.6, bf16[2,64,4096]{2,1,0:T(8,128)(2,1)} %bitcast.7, f32[512,4096]{1,0:T(8,128)} %earlier.1), custom_call_target="tpu_custom_call" | custom-call | tf_op jit(solution)/shard_map/features/pallas_call | solution.py:268
  20.5 3.5 %gram.1 = f32[512,4096]{1,0:T(8,128)} custom-call(bf16[48,512]{1,0:T(8,128)(2,1)S(1)} %get-tuple-element.8.left, bf16[48,4096]{1,0:T(8,128)(2,1)S(1)} %get-tuple-element.9.right, f32[512,4096]{1,0:T(8,128)S(1)} %get-tuple-element.10.earlier), custom_call_target="tpu_custom_call" | custom-call | tf_op jit(solution)/shard_map/gram/pallas_call | solution.py:309

commit v4 on v3

v4 whole, which is shorter than its diff:
```python
import functools
import math

import jax
import jax.numpy as jnp
from jax import lax
from jax.experimental import pallas as pl
from jax.experimental.pallas import tpu as pltpu
from jax.sharding import PartitionSpec as P

MESH = pl.DeviceIdType.MESH
LANES = 128
PIECES = ((2, 2, 2, 2), (2, 2, 2, 2))
FIRST = 2
TURN = 1


def split(x):
    hi = x.astype(jnp.bfloat16)
    lo = (x - hi.astype(jnp.float32)).astype(jnp.bfloat16)
    return hi, lo


def feature_kernel(
    n, groups, count, scale,
    act, grad, p_in, p_out, earlier,
    left, right, held,
    act_v, grad_v, in_v, out_v,
    theirs, mine, arrived, pieces, own, cols, row,
    load_sem, pair_sem, send_sem, recv_sem, col_recv, row_send, row_recv, held_sem,
):
    s = lax.axis_index("section")
    d = lax.axis_index("dp")
    chips = n // 2
    core = s % 2
    chip = s // 2
    partner = s + 1 - 2 * core

    draws, width, k_in = p_in.shape
    k_out = p_out.shape[1]
    tokens = act.shape[0]
    length = tokens // count

    parts = len(PIECES)
    part_count = count // parts
    part_tokens = part_count * length
    k_half = k_out // 2
    half_rows = k_half * part_count

    loads, spans = [], []
    for p, shares in enumerate(PIECES):
        rs = slice(p * part_tokens, (p + 1) * part_tokens)
        spans.append([])
        at = 0
        for share in shares:
            depth = width * share // sum(shares)
            cs = slice(at, at + depth)
            at += depth
            sem = load_sem.at[len(loads)]
            copies = []
            if p == 0:
                copies.append(pltpu.make_async_copy(p_in.at[:, cs], in_v.at[:, cs], sem))
                copies.append(pltpu.make_async_copy(p_out.at[:, :, cs], out_v.at[:, :, cs], sem))
            copies.append(pltpu.make_async_copy(act.at[rs, cs], act_v.at[rs, cs], sem))
            copies.append(pltpu.make_async_copy(grad.at[rs, cs], grad_v.at[rs, cs], sem))
            taken = depth * (2 * part_tokens + (draws * (k_in + k_out) if p == 0 else 0)) // width
            whole = pltpu.make_async_copy(act.at[pl.ds(0, taken)], act_v.at[pl.ds(0, taken)], sem)
            spans[p].append((cs, whole))
            loads.append(copies)

    def start(some):
        for copies in some:
            for copy in copies:
                copy.start()

    start(loads[:FIRST])
    barrier = pltpu.get_barrier_semaphore()
    for g in range(groups):
        for i in range(n):
            pl.semaphore_signal(barrier, inc=1, device_id={"section": i, "dp": g}, device_id_type=MESH)
    start(loads[FIRST:])

    def project(p, pieces_now, sums):
        rs = slice(p * part_tokens, (p + 1) * part_tokens)
        for cs, whole in pieces_now:
            whole.wait()
            weights = jnp.concatenate([in_v[i, cs, :] for i in range(draws)], axis=1)
            term_in = jnp.dot(act_v[rs, cs], weights, preferred_element_type=jnp.float32)
            weights = out_v[:, :, cs].reshape(draws * k_out, cs.stop - cs.start)
            term_out = lax.dot_general(
                grad_v[rs, cs], weights, (((1,), (1,)), ((), ())), preferred_element_type=jnp.float32
            )
            sums = (term_in, term_out) if sums is None else (sums[0] + term_in, sums[1] + term_out)
        return sums

    def factors(sums):
        low_in = sums[0].astype(jnp.bfloat16)
        found = []
        for e in range(part_count):
            ts = slice(e * length, (e + 1) * length)
            lhs = jnp.concatenate([sums[1][ts, i * k_out:(i + 1) * k_out] for i in range(draws)], axis=0)
            rhs = jnp.concatenate([low_in[ts, i * k_in:(i + 1) * k_in] for i in range(draws)], axis=0)
            found.append((lhs.T.astype(jnp.bfloat16), rhs))
        return found

    def terms(found, which, p, into):
        for e, (lhs, rhs) in enumerate(found):
            lhs = jnp.where(which == 0, lhs[:k_half], lhs[k_half:])
            into[p, pl.ds(e, k_half, stride=part_count), :] = jnp.dot(lhs, rhs, preferred_element_type=jnp.float32)

    def remote(src, dst, ssem, rsem, section, dp):
        return pltpu.make_async_remote_copy(
            src_ref=src, dst_ref=dst, send_sem=ssem, recv_sem=rsem,
            device_id={"section": section, "dp": dp}, device_id_type=MESH,
        )

    def across(c, i):
        bit = 1
        while bit < chips:
            if i & bit:
                c = c + bit * (1 - 2 * ((c // bit) % 2))
            bit *= 2
        return c

    k_chunk = k_half // chips
    rows = k_chunk * part_count
    turns = [2 * (m ^ m // 2) + b for m in range(1, chips // 2) for b in (0, 1)] + [1]

    def chunk(c):
        return pl.ds(pl.multiple_of(c * rows, rows), rows)

    def swap(p):
        return remote(theirs.at[p], arrived.at[p], send_sem.at[4], pair_sem.at[p], partner, d)

    def scatter(p):
        for slot, i in enumerate(turns):
            to = across(chip, i)
            ks = chunk(to)
            mine[p, ks, :] = mine[p, ks, :] + arrived[p, ks, :]
            remote(mine.at[p, ks], pieces.at[p, slot], send_sem.at[0], recv_sem.at[p], 2 * to + core, d).start()

    sums = []
    for p in range(parts):
        late = p == parts - 1
        early = spans[p][:TURN] if late else spans[p]
        total = project(p, early, None)
        if late:
            pl.semaphore_wait(barrier, n * groups)
            for o in range(p):
                swap(o).start()
            total = project(p, spans[p][TURN:], total)
        found = factors(total)
        terms(found, 1 - core, p, theirs)
        if late:
            swap(p).start()
            for o in range(p):
                swap(o).wait_recv()
                scatter(o)
        terms(found, core, p, mine)
    swap(parts - 1).wait_recv()
    scatter(parts - 1)
    hold = pltpu.make_async_copy(earlier, held, held_sem)
    hold.start()

    per_group = n // groups
    q = core * chips + chip
    own_slot = q % per_group
    home = q // per_group
    at_home = home == d

    cross = jnp.logical_not(at_home)

    def gather(p):
        ps = pl.ds(p * rows, rows)

        def col_copy(to):
            return remote(own.at[ps], cols.at[own_slot, d, ps], send_sem.at[1], col_recv.at[own_slot], to, home)

        for i in range(chips - 1):
            col_copy(2 * jnp.where(chip <= i, i + 1, i) + core).start()

        @pl.when(at_home)
        def _():
            col_copy(partner).start()
            cols[own_slot, d, ps] = own[ps]

        @pl.when(cross)
        def _():
            col_copy(s).start()

        for g in range(groups):
            here = jnp.logical_and(q == s, d == g)

            @pl.when(jnp.logical_and(home != g, jnp.logical_not(here)))
            def _():
                remote(own.at[ps], row.at[d, ps], row_send.at[g], row_recv.at[d], q, g).start()

            @pl.when(jnp.logical_and(home != g, here))
            def _():
                row[d, ps] = own[ps]

    for p in range(parts):
        ks = chunk(chip)
        total = mine[p, ks, :] + arrived[p, ks, :]
        remote(pieces.at[p], pieces.at[p], send_sem.at[0], recv_sem.at[p], partner, d).wait_recv()
        for i in range(chips - 1):
            total = total + pieces[p, i]
        own[p * rows:(p + 1) * rows, :] = total
        gather(p)

    def rows_of(ref, k):
        starts = [p * rows + k * part_count for p in range(parts)]
        return jnp.concatenate([ref[g, at:at + part_count] for g in range(groups) for at in starts], axis=0)

    def forward(j, lo, size, sem):
        ref = cols.at[j, pl.ds(lo, size)]
        return remote(ref, ref, send_sem.at[sem], col_recv.at[j], partner, d)

    passes = d * per_group // chips == core
    for i in range(per_group):
        j = across(chip, i) % per_group
        mixed = d * per_group + j == q

        @pl.when(jnp.logical_not(mixed))
        def _():
            forward(j, 0, groups, 2).wait_recv()

            @pl.when(passes)
            def _():
                forward(j, 0, groups, 2).start()

        @pl.when(mixed)
        def _():
            forward(j, 0, groups - 1, 3).wait_recv()
            for g in range(groups):

                @pl.when(d != g)
                def _():
                    forward(j, g, 1, 3).start()

        for k in range(k_chunk):
            hi, lo = split(rows_of(cols.at[j], k))
            at = pl.multiple_of((j * k_chunk + k) * LANES, LANES)
            right[:, pl.ds(at, LANES)] = jnp.concatenate([hi, hi, lo], axis=0)

    for g in range(groups):

        @pl.when(jnp.logical_and(s // per_group != d, jnp.logical_or(q != s, d != g)))
        def _():
            remote(own, row.at[g], row_send.at[g], row_recv.at[g], q, d).wait_recv()

    @pl.when(s // per_group == d)
    def _():
        row[...] = cols[s % per_group]

    for k in range(k_chunk):
        hi, lo = split(rows_of(row, k) * scale)
        left[:, k * LANES:(k + 1) * LANES] = jnp.concatenate([hi, lo, hi], axis=0)

    hold.wait()
    remote(theirs, theirs, send_sem.at[4], recv_sem.at[0], partner, d).wait_send()
    remote(pieces, pieces, send_sem.at[0], recv_sem.at[0], partner, d).wait_send()
    remote(arrived, arrived, send_sem.at[1], recv_sem.at[0], partner, d).wait_send()
    for g in range(groups):

        @pl.when(jnp.logical_and(home != g, jnp.logical_or(q != s, d != g)))
        def _():
            remote(own, row.at[d], row_send.at[g], row_recv.at[d], q, g).wait_send()

    def forwarded(count, sem):
        ref = cols.at[pl.ds(0, count)]
        remote(ref, ref, send_sem.at[sem], recv_sem.at[0], partner, d).wait_send()

    @pl.when(at_home)
    def _():
        forwarded(per_group - 1, 2)
        forward(0, 0, groups - 1, 3).wait_send()

    @pl.when(jnp.logical_and(passes, cross))
    def _():
        forwarded(per_group, 2)


def gram_kernel(tiles, left, right, earlier, out, tile_v, sem):
    height = earlier.shape[0] // tiles
    lhs = left[...].T
    copies = []
    for i in range(tiles):
        rs = slice(i * height, (i + 1) * height)
        tile_v[rs, :] = earlier[rs, :] + jnp.dot(lhs[rs], right[...], preferred_element_type=jnp.float32)
        copy = pltpu.make_async_copy(
            tile_v.at[pl.ds(i * height, height)], out.at[pl.ds(i * height, height)], sem.at[0]
        )
        copy.start()
        copies.append(copy)
    pltpu.make_async_copy(tile_v, out, sem.at[0]).wait()


def per_device(activations, out_grads, proj_in, proj_out, earlier_gram):
    n = lax.axis_size("section")
    groups = lax.axis_size("dp")
    _, count, length, width = activations.shape
    _, draws, _, k_in = proj_in.shape
    k_out = proj_out.shape[2]
    tokens = count * length
    examples = count * groups
    scale = 1.0 / (length * n * draws) / examples
    row_width, col_width = earlier_gram.shape
    chips = n // 2
    k_half = k_out // 2
    k_chunk = k_half // chips
    per_group = n // groups
    parts = len(PIECES)
    half_rows = k_half * (count // parts)
    rows = half_rows // chips
    any_spec = pl.BlockSpec(memory_space=pl.ANY)
    vmem_spec = pl.BlockSpec(memory_space=pltpu.VMEM)
    f32, bf16 = jnp.float32, jnp.bfloat16
    dma = pltpu.SemaphoreType.DMA

    left, right, held = pl.pallas_call(
        functools.partial(feature_kernel, n, groups, count, scale),
        out_shape=(
            pltpu.VMEM((3 * examples, row_width), bf16),
            pltpu.VMEM((3 * examples, col_width), bf16),
            pltpu.VMEM((row_width, col_width), f32),
        ),
        in_specs=[any_spec] * 5,
        out_specs=(vmem_spec, vmem_spec, vmem_spec),
        scratch_shapes=[
            pltpu.VMEM((tokens, width), bf16),
            pltpu.VMEM((tokens, width), bf16),
            pltpu.VMEM((draws, width, k_in), bf16),
            pltpu.VMEM((draws, k_out, width), bf16),
            pltpu.VMEM((parts, half_rows, k_in), f32),
            pltpu.VMEM((parts, half_rows, k_in), f32),
            pltpu.VMEM((parts, half_rows, k_in), f32),
            pltpu.VMEM((parts, chips - 1, rows, k_in), f32),
            pltpu.VMEM((parts * rows, k_in), f32),
            pltpu.VMEM((per_group, groups, parts * rows, k_in), f32),
            pltpu.VMEM((groups, parts * rows, k_in), f32),
            dma((sum(len(shares) for shares in PIECES),)),
            dma((parts,)),
            dma((5,)),
            dma((parts,)),
            dma((per_group,)),
            dma((groups,)),
            dma((groups,)),
            dma,
        ],
        compiler_params=pltpu.CompilerParams(
            collective_id=0, has_side_effects=True, vmem_limit_bytes=52 << 20
        ),
        name="features",
    )(
        activations.reshape(tokens, width),
        out_grads.reshape(tokens, width),
        proj_in[0],
        proj_out[0],
        earlier_gram,
    )
    tiles = 16
    return pl.pallas_call(
        functools.partial(gram_kernel, tiles),
        out_shape=jax.ShapeDtypeStruct((row_width, col_width), f32),
        in_specs=[vmem_spec, vmem_spec, vmem_spec],
        out_specs=any_spec,
        scratch_shapes=[pltpu.VMEM((row_width, col_width), f32), dma((1,))],
        compiler_params=pltpu.CompilerParams(vmem_limit_bytes=28 << 20),
        name="gram",
    )(left, right, held)


def solution(mesh):
    return jax.shard_map(
        per_device,
        mesh=mesh,
        in_specs=(
            P("section", "dp", None, None),
            P("section", "dp", None, None),
            P("section", None, None, None),
            P("section", None, None, None),
            P("section", "dp"),
        ),
        out_specs=P("section", "dp"),
        check_vma=False,
    )
```

time: 24.2 us -> 23.3 us (0.963)
  Pallas kernels: 24 us -> 23.1 us
    pallas_call x1, Pallas kernels: 20.5 us -> 19.6 us  [per_device(): pl.pallas_call(functools.partial(feature_kernel, n, groups, count, scale)...]
where the time goes in v4:
time: 23.3 us; the launch traced here: 23.1 us
  Pallas kernels  23.1 us (99%)
    pallas_call x1, Pallas kernels, per_device(): pl.pallas_call(functools.partial(feature_kernel, n, groups, count, scale)...  19.6 us
    pallas_call x1, Pallas kernels, per_device(): pl.pallas_call(functools.partial(gram_kernel, tiles), out_shape=jax.Shape...  3.54 us

profile of v4, /device:TPU:0, one launch (start us, length us, event | category | flops | bytes accessed | tf_op | source)
XLA Modules:
  0.0 23.1 jit_solution(11758815276326855282)
XLA Ops:
  0.0 19.6 %features.1 = (bf16[48,512]{1,0:T(8,128)(2,1)S(1)}, bf16[48,4096]{1,0:T(8,128)(2,1)S(1)}, f32[512,4096]{1,0:T(8,128)S(1)}) custom-call(bf16[512,4096]{1,0:T(8,128)(2,1)} %bitcast.4, bf16[512,4096]{1,0:T(8,128)(2,1)} %bitcast.5, bf16[2,4096,128]{2,1,0:T(8,128)(2,1)} %bitcast.6, bf16[2,64,4096]{2,1,0:T(8,128)(2,1)} %bitcast.7, f32[512,4096]{1,0:T(8,128)} %earlier.1), custom_call_target="tpu_custom_call" | custom-call | tf_op jit(solution)/shard_map/features/pallas_call | solution.py:321
  19.6 3.5 %gram.1 = f32[512,4096]{1,0:T(8,128)} custom-call(bf16[48,512]{1,0:T(8,128)(2,1)S(1)} %get-tuple-element.8.left, bf16[48,4096]{1,0:T(8,128)(2,1)S(1)} %get-tuple-element.9.right, f32[512,4096]{1,0:T(8,128)S(1)} %get-tuple-element.10.earlier), custom_call_target="tpu_custom_call" | custom-call | tf_op jit(solution)/shard_map/gram/pallas_call | solution.py:363

commit v5 on v4

--- a/solution.py
+++ b/solution.py
@@ -169,6 +169,8 @@
     at_home = home == d
 
     cross = jnp.logical_not(at_home)
+    direct = jnp.logical_and(chip == 0, d == 0)
+    twice = jnp.logical_and(home == 0, jnp.logical_not(direct))
 
     def gather(p):
         ps = pl.ds(p * rows, rows)
@@ -176,17 +178,19 @@
         def col_copy(to):
             return remote(own.at[ps], cols.at[own_slot, d, ps], send_sem.at[1], col_recv.at[own_slot], to, home)
 
-        for i in range(chips - 1):
-            col_copy(2 * jnp.where(chip <= i, i + 1, i) + core).start()
+        for i in range(chips):
+            col_copy(jnp.where(jnp.logical_and(at_home, chip == i), partner, 2 * i + core)).start()
+            if i == 0:
+
+                @pl.when(twice)
+                def _():
+                    remote(
+                        own.at[ps], cols.at[own_slot, d, ps], send_sem.at[5], col_recv.at[own_slot], 1 - core, home
+                    ).start()
 
         @pl.when(at_home)
         def _():
-            col_copy(partner).start()
             cols[own_slot, d, ps] = own[ps]
-
-        @pl.when(cross)
-        def _():
-            col_copy(s).start()
 
         for g in range(groups):
             here = jnp.logical_and(q == s, d == g)
@@ -216,7 +220,7 @@
         ref = cols.at[j, pl.ds(lo, size)]
         return remote(ref, ref, send_sem.at[sem], col_recv.at[j], partner, d)
 
-    passes = d * per_group // chips == core
+    passes = jnp.logical_and(d * per_group // chips == core, jnp.logical_not(direct))
     for i in range(per_group):
         j = across(chip, i) % per_group
         mixed = d * per_group + j == q
@@ -234,7 +238,7 @@
             forward(j, 0, groups - 1, 3).wait_recv()
             for g in range(groups):
 
-                @pl.when(d != g)
+                @pl.when(jnp.logical_and(passes, d != g))
                 def _():
                     forward(j, g, 1, 3).start()
 
@@ -271,7 +275,11 @@
         ref = cols.at[pl.ds(0, count)]
         remote(ref, ref, send_sem.at[sem], recv_sem.at[0], partner, d).wait_send()
 
-    @pl.when(at_home)
+    @pl.when(twice)
+    def _():
+        remote(own, own, send_sem.at[5], recv_sem.at[0], partner, d).wait_send()
+
+    @pl.when(jnp.logical_and(passes, at_home))
     def _():
         forwarded(per_group - 1, 2)
         forward(0, 0, groups - 1, 3).wait_send()
@@ -341,7 +349,7 @@
             pltpu.VMEM((groups, parts * rows, k_in), f32),
             dma((sum(len(shares) for shares in PIECES),)),
             dma((parts,)),
-            dma((5,)),
+            dma((6,)),
             dma((parts,)),
             dma((per_group,)),
             dma((groups,)),

time: 23.3 us -> 22.8 us (0.979); the launches traced: 23.1 us -> 22.4 us
  Pallas kernels: 23.1 us -> 22.3 us
    pallas_call x1, Pallas kernels: 19.6 us -> 18.8 us  [per_device(): pl.pallas_call(functools.partial(feature_kernel, n, groups, count, scale)...]
where the time goes in v5:
time: 22.8 us; the launch traced here: 22.4 us
  Pallas kernels  22.3 us (98%)
    pallas_call x1, Pallas kernels, per_device(): pl.pallas_call(functools.partial(feature_kernel, n, groups, count, scale)...  18.8 us
    pallas_call x1, Pallas kernels, per_device(): pl.pallas_call(functools.partial(gram_kernel, tiles), out_shape=jax.Shape...  3.54 us

profile of v5, /device:TPU:0, one launch (start us, length us, event | category | flops | bytes accessed | tf_op | source)
XLA Modules:
  0.0 22.4 jit_solution(11637228227402808373)
XLA Ops:
  0.0 18.8 %features.1 = (bf16[48,512]{1,0:T(8,128)(2,1)S(1)}, bf16[48,4096]{1,0:T(8,128)(2,1)S(1)}, f32[512,4096]{1,0:T(8,128)S(1)}) custom-call(bf16[512,4096]{1,0:T(8,128)(2,1)} %bitcast.4, bf16[512,4096]{1,0:T(8,128)(2,1)} %bitcast.5, bf16[2,4096,128]{2,1,0:T(8,128)(2,1)} %bitcast.6, bf16[2,64,4096]{2,1,0:T(8,128)(2,1)} %bitcast.7, f32[512,4096]{1,0:T(8,128)} %earlier.1), custom_call_target="tpu_custom_call" | custom-call | tf_op jit(solution)/shard_map/features/pallas_call | solution.py:329
  18.8 3.5 %gram.1 = f32[512,4096]{1,0:T(8,128)} custom-call(bf16[48,512]{1,0:T(8,128)(2,1)S(1)} %get-tuple-element.8.left, bf16[48,4096]{1,0:T(8,128)(2,1)S(1)} %get-tuple-element.9.right, f32[512,4096]{1,0:T(8,128)S(1)} %get-tuple-element.10.earlier), custom_call_target="tpu_custom_call" | custom-call | tf_op jit(solution)/shard_map/gram/pallas_call | solution.py:371

commit v6 on v5

--- a/solution.py
+++ b/solution.py
@@ -13,6 +13,7 @@
 PIECES = ((2, 2, 2, 2), (2, 2, 2, 2))
 FIRST = 2
 TURN = 1
+TILES = (1, 1, 2, 4, 4, 4, 4, 4, 4, 2, 1, 1)
 
 
 def split(x):
@@ -179,8 +180,9 @@
             return remote(own.at[ps], cols.at[own_slot, d, ps], send_sem.at[1], col_recv.at[own_slot], to, home)
 
         for i in range(chips):
-            col_copy(jnp.where(jnp.logical_and(at_home, chip == i), partner, 2 * i + core)).start()
-            if i == 0:
+            to = jnp.where(core == 0, i, chips - 1 - i)
+            col_copy(jnp.where(jnp.logical_and(at_home, chip == to), partner, 2 * to + core)).start()
+            if i == 1:
 
                 @pl.when(twice)
                 def _():
@@ -289,19 +291,16 @@
         forwarded(per_group, 2)
 
 
-def gram_kernel(tiles, left, right, earlier, out, tile_v, sem):
-    height = earlier.shape[0] // tiles
+def gram_kernel(left, right, earlier, out, tile_v, sem):
     lhs = left[...].T
-    copies = []
-    for i in range(tiles):
-        rs = slice(i * height, (i + 1) * height)
+    at = 0
+    for share in TILES:
+        height = earlier.shape[0] * share // sum(TILES)
+        rs = slice(at, at + height)
         tile_v[rs, :] = earlier[rs, :] + jnp.dot(lhs[rs], right[...], preferred_element_type=jnp.float32)
-        copy = pltpu.make_async_copy(
-            tile_v.at[pl.ds(i * height, height)], out.at[pl.ds(i * height, height)], sem.at[0]
-        )
-        copy.start()
-        copies.append(copy)
-    pltpu.make_async_copy(tile_v, out, sem.at[0]).wait()
+        pltpu.make_async_copy(tile_v.at[rs], out.at[rs], sem).start()
+        at += height
+    pltpu.make_async_copy(tile_v, out, sem).wait()
 
 
 def per_device(activations, out_grads, proj_in, proj_out, earlier_gram):
@@ -367,13 +366,12 @@
         proj_out[0],
         earlier_gram,
     )
-    tiles = 16
     return pl.pallas_call(
-        functools.partial(gram_kernel, tiles),
+        gram_kernel,
         out_shape=jax.ShapeDtypeStruct((row_width, col_width), f32),
         in_specs=[vmem_spec, vmem_spec, vmem_spec],
         out_specs=any_spec,
-        scratch_shapes=[pltpu.VMEM((row_width, col_width), f32), dma((1,))],
+        scratch_shapes=[pltpu.VMEM((row_width, col_width), f32), dma],
         compiler_params=pltpu.CompilerParams(vmem_limit_bytes=28 << 20),
         name="gram",
     )(left, right, held)

time: 22.8 us -> 22.6 us (level); the launches traced: 22.4 us -> 22.4 us
  no operation moved by 1% of the time
where the time goes in v6:
time: 22.6 us; the launch traced here: 22.4 us
  Pallas kernels  22.4 us (99%)
    pallas_call x1, Pallas kernels, per_device(): pl.pallas_call(functools.partial(feature_kernel, n, groups, count, scale)...  18.9 us
    pallas_call x1, Pallas kernels, per_device(): pl.pallas_call(gram_kernel, out_shape=jax.ShapeDtypeStruct((row_width, co...  3.53 us

profile of v6, /device:TPU:0, one launch (start us, length us, event | category | flops | bytes accessed | tf_op | source)
XLA Modules:
  0.0 22.4 jit_solution(13515512739953191935)
XLA Ops:
  0.0 18.9 %features.1 = (bf16[48,512]{1,0:T(8,128)(2,1)S(1)}, bf16[48,4096]{1,0:T(8,128)(2,1)S(1)}, f32[512,4096]{1,0:T(8,128)S(1)}) custom-call(bf16[512,4096]{1,0:T(8,128)(2,1)} %bitcast.4, bf16[512,4096]{1,0:T(8,128)(2,1)} %bitcast.5, bf16[2,4096,128]{2,1,0:T(8,128)(2,1)} %bitcast.6, bf16[2,64,4096]{2,1,0:T(8,128)(2,1)} %bitcast.7, f32[512,4096]{1,0:T(8,128)} %earlier.1), custom_call_target="tpu_custom_call" | custom-call | tf_op jit(solution)/shard_map/features/pallas_call | solution.py:328
  18.9 3.5 %gram.1 = f32[512,4096]{1,0:T(8,128)} custom-call(bf16[48,512]{1,0:T(8,128)(2,1)S(1)} %get-tuple-element.8.left, bf16[48,4096]{1,0:T(8,128)(2,1)S(1)} %get-tuple-element.9.right, f32[512,4096]{1,0:T(8,128)S(1)} %get-tuple-element.10.earlier), custom_call_target="tpu_custom_call" | custom-call | tf_op jit(solution)/shard_map/gram/pallas_call | solution.py:369

commit v7 on v6

--- a/solution.py
+++ b/solution.py
@@ -28,7 +28,7 @@
     left, right, held,
     act_v, grad_v, in_v, out_v,
     theirs, mine, arrived, pieces, own, cols, row,
-    load_sem, pair_sem, send_sem, recv_sem, col_recv, row_send, row_recv, held_sem,
+    load_sem, pair_sem, recv_sem, col_recv, row_send, row_recv, held_sem,
 ):
     s = lax.axis_index("section")
     d = lax.axis_index("dp")
@@ -131,14 +131,14 @@
         return pl.ds(pl.multiple_of(c * rows, rows), rows)
 
     def swap(p):
-        return remote(theirs.at[p], arrived.at[p], send_sem.at[4], pair_sem.at[p], partner, d)
+        return remote(theirs.at[p], arrived.at[p], load_sem.at[0], pair_sem.at[p], partner, d)
 
     def scatter(p):
         for slot, i in enumerate(turns):
             to = across(chip, i)
             ks = chunk(to)
             mine[p, ks, :] = mine[p, ks, :] + arrived[p, ks, :]
-            remote(mine.at[p, ks], pieces.at[p, slot], send_sem.at[0], recv_sem.at[p], 2 * to + core, d).start()
+            remote(mine.at[p, ks], pieces.at[p, slot], load_sem.at[4], recv_sem.at[p], 2 * to + core, d).start()
 
     sums = []
     for p in range(parts):
@@ -177,7 +177,7 @@
         ps = pl.ds(p * rows, rows)
 
         def col_copy(to):
-            return remote(own.at[ps], cols.at[own_slot, d, ps], send_sem.at[1], col_recv.at[own_slot], to, home)
+            return remote(own.at[ps], cols.at[own_slot, d, ps], load_sem.at[1], col_recv.at[own_slot], to, home)
 
         for i in range(chips):
             to = jnp.where(core == 0, i, chips - 1 - i)
@@ -187,7 +187,7 @@
                 @pl.when(twice)
                 def _():
                     remote(
-                        own.at[ps], cols.at[own_slot, d, ps], send_sem.at[5], col_recv.at[own_slot], 1 - core, home
+                        own.at[ps], cols.at[own_slot, d, ps], load_sem.at[5], col_recv.at[own_slot], 1 - core, home
                     ).start()
 
         @pl.when(at_home)
@@ -208,7 +208,7 @@
     for p in range(parts):
         ks = chunk(chip)
         total = mine[p, ks, :] + arrived[p, ks, :]
-        remote(pieces.at[p], pieces.at[p], send_sem.at[0], recv_sem.at[p], partner, d).wait_recv()
+        remote(pieces.at[p], pieces.at[p], load_sem.at[4], recv_sem.at[p], partner, d).wait_recv()
         for i in range(chips - 1):
             total = total + pieces[p, i]
         own[p * rows:(p + 1) * rows, :] = total
@@ -220,7 +220,7 @@
 
     def forward(j, lo, size, sem):
         ref = cols.at[j, pl.ds(lo, size)]
-        return remote(ref, ref, send_sem.at[sem], col_recv.at[j], partner, d)
+        return remote(ref, ref, load_sem.at[sem], col_recv.at[j], partner, d)
 
     passes = jnp.logical_and(d * per_group // chips == core, jnp.logical_not(direct))
     for i in range(per_group):
@@ -264,9 +264,9 @@
         left[:, k * LANES:(k + 1) * LANES] = jnp.concatenate([hi, lo, hi], axis=0)
 
     hold.wait()
-    remote(theirs, theirs, send_sem.at[4], recv_sem.at[0], partner, d).wait_send()
-    remote(pieces, pieces, send_sem.at[0], recv_sem.at[0], partner, d).wait_send()
-    remote(arrived, arrived, send_sem.at[1], recv_sem.at[0], partner, d).wait_send()
+    remote(theirs, theirs, load_sem.at[0], recv_sem.at[0], partner, d).wait_send()
+    remote(pieces, pieces, load_sem.at[4], recv_sem.at[0], partner, d).wait_send()
+    remote(arrived, arrived, load_sem.at[1], recv_sem.at[0], partner, d).wait_send()
     for g in range(groups):
 
         @pl.when(jnp.logical_and(home != g, jnp.logical_or(q != s, d != g)))
@@ -275,11 +275,11 @@
 
     def forwarded(count, sem):
         ref = cols.at[pl.ds(0, count)]
-        remote(ref, ref, send_sem.at[sem], recv_sem.at[0], partner, d).wait_send()
+        remote(ref, ref, load_sem.at[sem], recv_sem.at[0], partner, d).wait_send()
 
     @pl.when(twice)
     def _():
-        remote(own, own, send_sem.at[5], recv_sem.at[0], partner, d).wait_send()
+        remote(own, own, load_sem.at[5], recv_sem.at[0], partner, d).wait_send()
 
     @pl.when(jnp.logical_and(passes, at_home))
     def _():
@@ -346,9 +346,8 @@
             pltpu.VMEM((parts * rows, k_in), f32),
             pltpu.VMEM((per_group, groups, parts * rows, k_in), f32),
             pltpu.VMEM((groups, parts * rows, k_in), f32),
-            dma((sum(len(shares) for shares in PIECES),)),
+            dma((max(6, sum(len(shares) for shares in PIECES)),)),
             dma((parts,)),
-            dma((6,)),
             dma((parts,)),
             dma((per_group,)),
             dma((groups,)),

time: 22.6 us -> 22.5 us (level)
  no operation moved by 1% of the time
where the time goes in v7:
time: 22.5 us; the launch traced here: 22.3 us
  Pallas kernels  22.3 us (99%)
    pallas_call x1, Pallas kernels, per_device(): pl.pallas_call(functools.partial(feature_kernel, n, groups, count, scale)...  18.8 us
    pallas_call x1, Pallas kernels, per_device(): pl.pallas_call(gram_kernel, out_shape=jax.ShapeDtypeStruct((row_width, co...  3.51 us

profile of v7, /device:TPU:0, one launch (start us, length us, event | category | flops | bytes accessed | tf_op | source)
XLA Modules:
  0.0 22.3 jit_solution(10351546616941313742)
XLA Ops:
  0.0 18.8 %features.1 = (bf16[48,512]{1,0:T(8,128)(2,1)S(1)}, bf16[48,4096]{1,0:T(8,128)(2,1)S(1)}, f32[512,4096]{1,0:T(8,128)S(1)}) custom-call(bf16[512,4096]{1,0:T(8,128)(2,1)} %bitcast.4, bf16[512,4096]{1,0:T(8,128)(2,1)} %bitcast.5, bf16[2,4096,128]{2,1,0:T(8,128)(2,1)} %bitcast.6, bf16[2,64,4096]{2,1,0:T(8,128)(2,1)} %bitcast.7, f32[512,4096]{1,0:T(8,128)} %earlier.1), custom_call_target="tpu_custom_call" | custom-call | tf_op jit(solution)/shard_map/features/pallas_call | solution.py:328
  18.8 3.5 %gram.1 = f32[512,4096]{1,0:T(8,128)} custom-call(bf16[48,512]{1,0:T(8,128)(2,1)S(1)} %get-tuple-element.8.left, bf16[48,4096]{1,0:T(8,128)(2,1)S(1)} %get-tuple-element.9.right, f32[512,4096]{1,0:T(8,128)S(1)} %get-tuple-element.10.earlier), custom_call_target="tpu_custom_call" | custom-call | tf_op jit(solution)/shard_map/gram/pallas_call | solution.py:368

commit v8 on v7

--- a/solution.py
+++ b/solution.py
@@ -28,7 +28,7 @@
     left, right, held,
     act_v, grad_v, in_v, out_v,
     theirs, mine, arrived, pieces, own, cols, row,
-    load_sem, pair_sem, recv_sem, col_recv, row_send, row_recv, held_sem,
+    load_sem, pair_sem, recv_sem, col_recv, row_recv, held_sem,
 ):
     s = lax.axis_index("section")
     d = lax.axis_index("dp")
@@ -180,7 +180,7 @@
             return remote(own.at[ps], cols.at[own_slot, d, ps], load_sem.at[1], col_recv.at[own_slot], to, home)
 
         for i in range(chips):
-            to = jnp.where(core == 0, i, chips - 1 - i)
+            to = jnp.where(core == 0, i, (i + chips // 2) % chips)
             col_copy(jnp.where(jnp.logical_and(at_home, chip == to), partner, 2 * to + core)).start()
             if i == 1:
 
@@ -199,7 +199,7 @@
 
             @pl.when(jnp.logical_and(home != g, jnp.logical_not(here)))
             def _():
-                remote(own.at[ps], row.at[d, ps], row_send.at[g], row_recv.at[d], q, g).start()
+                remote(own.at[ps], row.at[d, ps], load_sem.at[6 + g], row_recv.at[d], q, g).start()
 
             @pl.when(jnp.logical_and(home != g, here))
             def _():
@@ -253,7 +253,7 @@
 
         @pl.when(jnp.logical_and(s // per_group != d, jnp.logical_or(q != s, d != g)))
         def _():
-            remote(own, row.at[g], row_send.at[g], row_recv.at[g], q, d).wait_recv()
+            remote(own, row.at[g], load_sem.at[6 + g], row_recv.at[g], q, d).wait_recv()
 
     @pl.when(s // per_group == d)
     def _():
@@ -271,7 +271,7 @@
 
         @pl.when(jnp.logical_and(home != g, jnp.logical_or(q != s, d != g)))
         def _():
-            remote(own, row.at[d], row_send.at[g], row_recv.at[d], q, g).wait_send()
+            remote(own, row.at[d], load_sem.at[6 + g], row_recv.at[d], q, g).wait_send()
 
     def forwarded(count, sem):
         ref = cols.at[pl.ds(0, count)]
@@ -346,11 +346,10 @@
             pltpu.VMEM((parts * rows, k_in), f32),
             pltpu.VMEM((per_group, groups, parts * rows, k_in), f32),
             pltpu.VMEM((groups, parts * rows, k_in), f32),
-            dma((max(6, sum(len(shares) for shares in PIECES)),)),
+            dma((max(6 + groups, sum(len(shares) for shares in PIECES)),)),
             dma((parts,)),
             dma((parts,)),
             dma((per_group,)),
-            dma((groups,)),
             dma((groups,)),
             dma,
         ],

time: 22.5 us -> 22.5 us (level)
  no operation moved by 1% of the time
where the time goes in v8:
time: 22.5 us; the launch traced here: 22.4 us
  Pallas kernels  22.3 us (99%)
    pallas_call x1, Pallas kernels, per_device(): pl.pallas_call(functools.partial(feature_kernel, n, groups, count, scale)...  18.8 us
    pallas_call x1, Pallas kernels, per_device(): pl.pallas_call(gram_kernel, out_shape=jax.ShapeDtypeStruct((row_width, co...  3.5 us

profile of v8, /device:TPU:0, one launch (start us, length us, event | category | flops | bytes accessed | tf_op | source)
XLA Modules:
  0.0 22.4 jit_solution(12212259893350617494)
XLA Ops:
  0.0 18.8 %features.1 = (bf16[48,512]{1,0:T(8,128)(2,1)S(1)}, bf16[48,4096]{1,0:T(8,128)(2,1)S(1)}, f32[512,4096]{1,0:T(8,128)S(1)}) custom-call(bf16[512,4096]{1,0:T(8,128)(2,1)} %bitcast.4, bf16[512,4096]{1,0:T(8,128)(2,1)} %bitcast.5, bf16[2,4096,128]{2,1,0:T(8,128)(2,1)} %bitcast.6, bf16[2,64,4096]{2,1,0:T(8,128)(2,1)} %bitcast.7, f32[512,4096]{1,0:T(8,128)} %earlier.1), custom_call_target="tpu_custom_call" | custom-call | tf_op jit(solution)/shard_map/features/pallas_call | solution.py:328
  18.8 3.5 %gram.1 = f32[512,4096]{1,0:T(8,128)} custom-call(bf16[48,512]{1,0:T(8,128)(2,1)S(1)} %get-tuple-element.8.left, bf16[48,4096]{1,0:T(8,128)(2,1)S(1)} %get-tuple-element.9.right, f32[512,4096]{1,0:T(8,128)S(1)} %get-tuple-element.10.earlier), custom_call_target="tpu_custom_call" | custom-call | tf_op jit(solution)/shard_map/gram/pallas_call | solution.py:367
